TPU v7x, 32 devices: a whole 2x2x4 slice. The times are simulated.
32 devices in a mesh: dp: 8 (over z, y), mp: 4 (over x, core).
Axes of the slice: x: 2, y: 2, z: 4, core: 2. Of those that a mesh axis runs over, the one named last changes fastest.
Arguments:
- patches: bfloat16 [16384, 1024], P('dp'), may hold values from -110 to 110
- dest_owner: int32 [1024], P('dp'), may hold values from 0 to 7, as said below
- dest_slot: int32 [1024], P('dp'), may hold values from 0 to 127
- packed_image: int32 [1024], P('dp'), may hold values from -1 to 15, as said below
- w_query: bfloat16 [1024, 1024], P(None, 'mp'), may hold values from -0.328125 to 0.328125
- w_key: bfloat16 [1024, 1024], P(None, 'mp'), may hold values from -1.9375 to 1.9375
- w_value: bfloat16 [1024, 1024], P(None, 'mp'), may hold values from -0.1875 to 0.1875
- w_out: bfloat16 [1024, 1024], P('mp'), may hold values from -0.1875 to 0.1875
Outputs:
- packed_out: bfloat16 [16384, 1024], P('dp', 'mp')
- pooled_out: bfloat16 [128, 1024], P('dp', 'mp')
Inputs may be any that keep to these rules, and one draw needn't show every extreme that they name: dest_owner and dest_slot take the tiles of all indices of dp one to one onto the 128 tile slots of every packed sequence; each index of dp holds exactly 16 tiles for each packed sequence. `packed_image`: in every packed sequence the images 0, 1, 2 and so on lie on consecutive tile slots from slot 0 in the order of their numbers, each on 8 to 16 slots; fewer than 16 slots stay empty after the last image and hold -1.
All inputs are finite; a program needn't handle non-finite values.
Results may differ from a plain program's by a relative error of at most 0.0075.
Values may be sent and summed in bfloat16 or wider, within the bound.
A program may use at most 128 MiB of HBM per device.

v0:
```python
import jax
import jax.numpy as jnp
from jax import lax
from jax.sharding import PartitionSpec as P

HEAD_DIM = 64
IMG_OWN = 16
EPSILON = 1e-06


def normalize(rows):
    values = rows.astype(jnp.float32)
    centred = values - jnp.mean(values, axis=-1, keepdims=True)
    spread = jnp.mean(centred * centred, axis=-1, keepdims=True)
    return (centred * lax.rsqrt(spread + EPSILON)).astype(jnp.bfloat16)


def attend(queries, key_rows, values, allowed, present):
    scores = jnp.einsum(
        "qhd,khd->hqk", queries, key_rows, preferred_element_type=jnp.float32
    ) * HEAD_DIM ** (-0.5)
    masked = jnp.where(allowed[None], scores, -1e30)
    peak = jnp.max(masked, axis=-1, keepdims=True)
    raised = jnp.where(allowed[None], jnp.exp(scores - peak), 0.0)
    denominator = jnp.sum(raised, axis=-1, keepdims=True)
    denominator = jnp.where(present[None, :, None], denominator, 1.0)
    weights = (raised / denominator).astype(jnp.bfloat16)
    return jnp.einsum("hqk,khd->qhd", weights, values, preferred_element_type=jnp.float32).astype(
        jnp.bfloat16
    )


def whole_rows(queries, key_rows, values, segment, present):
    count_rows = queries.shape[0]
    block_rows = min(512, count_rows)

    def one_block(step_index):
        first_row = step_index * block_rows
        query_part = lax.dynamic_slice_in_dim(queries, first_row, block_rows, 0)
        segment_part = lax.dynamic_slice_in_dim(segment, first_row, block_rows, 0)
        live_rows = lax.dynamic_slice_in_dim(present, first_row, block_rows, 0)
        allowed = (segment_part[:, None] == segment[None, :]) & live_rows[:, None]
        return attend(query_part, key_rows, values, allowed, live_rows)

    outcome = lax.map(one_block, jnp.arange(count_rows // block_rows, dtype=jnp.int32))
    return outcome.reshape(count_rows, -1)


def on_device(patches, dest_owner, dest_slot, packed_image, w_query, w_key, w_value, w_out):
    senders = lax.axis_size("dp")
    splits = lax.axis_size("mp")
    slot_count = dest_owner.shape[0]
    per_owner = slot_count // senders
    tile_size = patches.shape[0] // slot_count
    full_width = patches.shape[1]
    part_width = full_width // splits
    numbers = jnp.arange(slot_count, dtype=jnp.int32)
    same_owner = dest_owner[:, None] == dest_owner[None, :]
    ranking = jnp.sum(
        (same_owner & (numbers[None, :] < numbers[:, None])).astype(jnp.int32), axis=1
    )
    position = dest_owner * per_owner + ranking
    picked = position[None, :] == numbers[:, None]
    ordering = jnp.sum(jnp.where(picked, numbers[None, :], 0), axis=1)
    slot_sent = jnp.sum(jnp.where(picked, dest_slot[None, :], 0), axis=1)
    got_slot = lax.all_to_all(slot_sent, "dp", split_axis=0, concat_axis=0, tiled=True)
    arrive = jnp.sum(jnp.where(got_slot[None, :] == numbers[:, None], numbers[None, :], 0), axis=1)
    tile_data = patches.reshape(slot_count, tile_size, full_width)
    column_start = lax.axis_index("mp") * part_width
    own_part = lax.dynamic_slice_in_dim(tile_data, column_start, part_width, 2)
    outgoing = jnp.take(own_part, ordering, axis=0).reshape(slot_count * tile_size, part_width)
    incoming = lax.all_to_all(outgoing, "dp", split_axis=0, concat_axis=0, tiled=True)
    own_cols = jnp.take(
        incoming.reshape(slot_count, tile_size, part_width), arrive, axis=0
    ).reshape(slot_count * tile_size, part_width)
    full_rows = lax.all_gather(own_cols, "mp", axis=1, tiled=True)
    count_rows = slot_count * tile_size
    segment = jnp.repeat(packed_image, tile_size)
    present = segment >= 0
    normed = normalize(full_rows)
    head_count = w_query.shape[1] // HEAD_DIM
    queries = (
        jnp.dot(normed, w_query, preferred_element_type=jnp.float32)
        .astype(jnp.bfloat16)
        .reshape(count_rows, head_count, HEAD_DIM)
    )
    key_rows = (
        jnp.dot(normed, w_key, preferred_element_type=jnp.float32)
        .astype(jnp.bfloat16)
        .reshape(count_rows, head_count, HEAD_DIM)
    )
    values = (
        jnp.dot(normed, w_value, preferred_element_type=jnp.float32)
        .astype(jnp.bfloat16)
        .reshape(count_rows, head_count, HEAD_DIM)
    )
    attended = whole_rows(queries, key_rows, values, segment, present)
    head_term = jnp.dot(attended, w_out, preferred_element_type=jnp.float32)
    summed = lax.psum_scatter(
        head_term.astype(jnp.bfloat16), "mp", scatter_dimension=1, tiled=True
    ).astype(jnp.float32)
    result_rows = jnp.where(present[:, None], own_cols.astype(jnp.float32) + summed, 0.0)
    packed_out = result_rows.astype(jnp.bfloat16)
    labels = jnp.arange(IMG_OWN, dtype=jnp.int32)
    member = (segment[None, :] == labels[:, None]).astype(jnp.float32)
    sums = jnp.dot(member, result_rows, precision=lax.Precision.HIGHEST)
    image_rows = jnp.sum(member, axis=1)
    filled = image_rows > 0
    pooled = sums / jnp.maximum(image_rows, 1.0)[:, None]
    local_sum = jnp.sum(jnp.where(filled[:, None], pooled, 0.0), axis=0)
    local_count = jnp.sum(filled.astype(jnp.float32))
    grand_total, number = lax.psum((local_sum, local_count), "dp")
    centre = grand_total / number
    pooled_out = jnp.where(filled[:, None], pooled - centre[None, :], 0.0).astype(jnp.bfloat16)
    return (packed_out, pooled_out)


def solution(mesh):
    in_specs = (
        P("dp", None),
        P("dp"),
        P("dp"),
        P("dp"),
        P(None, "mp"),
        P(None, "mp"),
        P(None, "mp"),
        P("mp", None),
    )
    out_specs = (P("dp", "mp"), P("dp", "mp"))
    return jax.shard_map(
        on_device, mesh=mesh, in_specs=in_specs, out_specs=out_specs, check_vma=False
    )
```

profile of v0, /device:TPU:0, one launch (start us, length us, event | category | flops | bytes accessed | tf_op | source)
XLA Modules:
  0.0 283.8 jit_solution(2327120010386773633)
XLA Ops:
  7.2 0.9 convert_reduce_fusion.2
  8.1 0.7 multiply_add_fusion
  8.8 0.8 select_reduce_fusion.2
  9.5 0.7 all_to_all.14
  10.2 7.3 %all-to-all-start.1 = ((s32[8,16,1]{1,2,0:T(1,128)}), s32[8,16,1]{1,2,0:T(1,128)S(1)}, u32[]{:S(2)}, u32[]{:S(2)}) async-start(s32[8,16,1]{1,2,0:T(1,128)} %bitcast), calls=%async_computation.1 | async-start | bytes 8192 | tf_op jit(solution)/shard_map/all_to_all | solution.py:66
  17.5 1.3 constant_dynamic-slice_fusion
  18.9 0.6 gather_fusion
  19.5 1.2 broadcast_select_fusion.2
  20.7 3.2 %all-to-all-done.1 = s32[8,16,1]{1,2,0:T(1,128)S(1)} async-done(((s32[8,16,1]{1,2,0:T(1,128)}), s32[8,16,1]{1,2,0:T(1,128)S(1)}, u32[]{:S(2)}, u32[]{:S(2)}) %all-to-all-start.1) | async-done | bytes 544 | tf_op jit(solution)/shard_map/all_to_all | solution.py:66
  23.9 3.6 %all-to-all-start = ((bf16[8,256,256]{2,1,0:T(8,128)(2,1)}), bf16[8,256,256]{2,1,0:T(8,128)(2,1)S(1)}, u32[]{:S(2)}, u32[]{:S(2)}) async-start(bf16[8,256,256]{2,1,0:T(8,128)(2,1)} %bitcast.2), calls=%async_computation | async-start | bytes 2097152 | tf_op jit(solution)/shard_map/all_to_all | solution.py:72
  27.5 0.5 broadcast.115
  28.1 0.7 reduce.3
  28.7 0.1 eq.74
  28.8 0.1 select_reduce_fusion.1
  29.0 23.3 %all-to-all-done = bf16[8,256,256]{2,1,0:T(8,128)(2,1)S(1)} async-done(((bf16[8,256,256]{2,1,0:T(8,128)(2,1)}), bf16[8,256,256]{2,1,0:T(8,128)(2,1)S(1)}, u32[]{:S(2)}, u32[]{:S(2)}) %all-to-all-start) | async-done | bytes 1048608 | tf_op jit(solution)/shard_map/all_to_all | solution.py:72
  52.2 0.6 gather_fusion.1
  52.9 1.2 broadcast_select_fusion.1
  54.2 0.1 reshape.133
  54.3 33.8 %all-gather.2.cloned.1.call-done = bf16[2048,1024]{1,0:T(8,128)(2,1)} async-done(((bf16[2048,256]{1,0:T(8,128)(2,1)}), bf16[2048,1024]{1,0:T(8,128)(2,1)}) %all-gather.2.cloned.1.call-update) | async-done | bytes 4194320 | tf_op jit(solution)/shard_map/all_gather | solution.py:76
  88.1 3.0 %convert_reduce_fusion = f32[2048]{0:T(1024)S(1)} fusion(bf16[2048,1024]{1,0:T(8,128)(2,1)} %all-gather.2.cloned.1.call-done), kind=kLoop, calls=%fused_computation.27 | loop fusion | flops 4192256 | bytes 4202496 | tf_op jit(solution)/shard_map/reduce_sum | solution.py:13
  91.0 0.5 copy-done.1
  91.5 1.4 fusion.31
  92.9 1.1 fusion.32
  94.1 2.3 convolution_convert_fusion.3
  96.4 2.3 convolution_convert_fusion.2
  98.8 2.3 convolution_convert_fusion.1
  101.1 99.0 %while.11 = (s32[]{:T(128)}, bf16[4,512,4,64]{1,3,2,0:T(8,128)(2,1)S(1)}, s32[4]{0:T(128)S(1)}, s32[2048]{0:T(1024)S(1)}, pred[2048]{0:T(1024)(128)(4,1)S(1)}, /...) while((s32[]{:T(128)}, ...), condition=%wide.region_9.11_spmd.clone, body=%wide.region_6.0_spmd.clone.sunk | while | flops 1646399488 | bytes 40707776 | solution.py:45
  101.1 0.7 dynamic_slice.41
  102.4 0.1 dynamic_slice.43
  102.5 0.1 dynamic_slice.42
  102.7 0.1 eq.127
  102.8 0.8 compare_and_fusion.4
  103.5 13.5 %fusion.69 = (f32[4,512]{1,0:T(4,128)S(1)}, f32[4,512,2048]{2,1,0:T(8,128)}) fusion(pred[512,2048]{1,0:T(8,128)(4,1)S(1)} %compare_and_fusion.4, bf16[2048,4,64]{0,2,1:T(8,128)(2,1)} %get-tuple-element.191, bf16[2048,4,64]{0,2,1:T(8,128)(2,1)} %get-tuple-element.190, s32[]{:T(128)S(6)} %select_n.104), kind=kOutput, calls=%fused_computation.73.clone.1 | convolution fusion | flops 1098909696 | bytes 21505024 | tf_op jit(solution)/shard_map/while/body/eval_jaxpr/sub | solution.py:24
  117.0 8.7 %fusion.70 = bf16[4,512,4,64]{1,3,2,0:T(8,128)(2,1)S(1)} fusion(bf16[4,512,4,64]{1,3,2,0:T(8,128)(2,1)S(1)} %get-tuple-element.173, s32[]{:T(128)} %get-tuple-element.172, bf16[2048,4,64]{0,2,1:T(8,128)(2,1)} %get-tuple-element.192, f32[4,512,2048]{2,1,0:T(8,128)} %get-tuple-element.157, f32[4,512]{1,0:T(4,128)S(1)} %broadcast_select_fusion.4), kind=kOutput, calls=%fused_computation.17.clone.1 | convolution fusion | flops 545390592 | bytes 18096132 | tf_op jit(solution)/shard_map/while/body/eval_jaxpr/hqk,khd->qhd/dot_general | solution.py:28
  125.8 0.7 dynamic_slice.41
  127.2 0.1 dynamic_slice.43
  127.2 0.1 dynamic_slice.42
  127.4 0.1 eq.127
  127.5 0.8 compare_and_fusion.4
  128.3 13.5 %fusion.69 = (f32[4,512]{1,0:T(4,128)S(1)}, f32[4,512,2048]{2,1,0:T(8,128)}) fusion(pred[512,2048]{1,0:T(8,128)(4,1)S(1)} %compare_and_fusion.4, bf16[2048,4,64]{0,2,1:T(8,128)(2,1)} %get-tuple-element.191, bf16[2048,4,64]{0,2,1:T(8,128)(2,1)} %get-tuple-element.190, s32[]{:T(128)S(6)} %select_n.104), kind=kOutput, calls=%fused_computation.73.clone.1 | convolution fusion | flops 1098909696 | bytes 21505024 | tf_op jit(solution)/shard_map/while/body/eval_jaxpr/sub | solution.py:24
  141.8 8.7 %fusion.70 = bf16[4,512,4,64]{1,3,2,0:T(8,128)(2,1)S(1)} fusion(bf16[4,512,4,64]{1,3,2,0:T(8,128)(2,1)S(1)} %get-tuple-element.173, s32[]{:T(128)} %get-tuple-element.172, bf16[2048,4,64]{0,2,1:T(8,128)(2,1)} %get-tuple-element.192, f32[4,512,2048]{2,1,0:T(8,128)} %get-tuple-element.157, f32[4,512]{1,0:T(4,128)S(1)} %broadcast_select_fusion.4), kind=kOutput, calls=%fused_computation.17.clone.1 | convolution fusion | flops 545390592 | bytes 18096132 | tf_op jit(solution)/shard_map/while/body/eval_jaxpr/hqk,khd->qhd/dot_general | solution.py:28
  150.5 0.7 dynamic_slice.41
  151.9 0.1 dynamic_slice.43
  152.1 0.1 eq.127
  152.2 0.8 compare_and_fusion.4
  153.0 13.6 %fusion.69 = (f32[4,512]{1,0:T(4,128)S(1)}, f32[4,512,2048]{2,1,0:T(8,128)}) fusion(pred[512,2048]{1,0:T(8,128)(4,1)S(1)} %compare_and_fusion.4, bf16[2048,4,64]{0,2,1:T(8,128)(2,1)} %get-tuple-element.191, bf16[2048,4,64]{0,2,1:T(8,128)(2,1)} %get-tuple-element.190, s32[]{:T(128)S(6)} %select_n.104), kind=kOutput, calls=%fused_computation.73.clone.1 | convolution fusion | flops 1098909696 | bytes 21505024 | tf_op jit(solution)/shard_map/while/body/eval_jaxpr/sub | solution.py:24
  166.6 8.7 %fusion.70 = bf16[4,512,4,64]{1,3,2,0:T(8,128)(2,1)S(1)} fusion(bf16[4,512,4,64]{1,3,2,0:T(8,128)(2,1)S(1)} %get-tuple-element.173, s32[]{:T(128)} %get-tuple-element.172, bf16[2048,4,64]{0,2,1:T(8,128)(2,1)} %get-tuple-element.192, f32[4,512,2048]{2,1,0:T(8,128)} %get-tuple-element.157, f32[4,512]{1,0:T(4,128)S(1)} %broadcast_select_fusion.4), kind=kOutput, calls=%fused_computation.17.clone.1 | convolution fusion | flops 545390592 | bytes 18096132 | tf_op jit(solution)/shard_map/while/body/eval_jaxpr/hqk,khd->qhd/dot_general | solution.py:28
  175.3 0.7 dynamic_slice.41
  176.7 0.1 dynamic_slice.43
  176.9 0.1 eq.127
  177.0 0.8 compare_and_fusion.4
  177.8 13.5 %fusion.69 = (f32[4,512]{1,0:T(4,128)S(1)}, f32[4,512,2048]{2,1,0:T(8,128)}) fusion(pred[512,2048]{1,0:T(8,128)(4,1)S(1)} %compare_and_fusion.4, bf16[2048,4,64]{0,2,1:T(8,128)(2,1)} %get-tuple-element.191, bf16[2048,4,64]{0,2,1:T(8,128)(2,1)} %get-tuple-element.190, s32[]{:T(128)S(6)} %select_n.104), kind=kOutput, calls=%fused_computation.73.clone.1 | convolution fusion | flops 1098909696 | bytes 21505024 | tf_op jit(solution)/shard_map/while/body/eval_jaxpr/sub | solution.py:24
  191.3 8.7 %fusion.70 = bf16[4,512,4,64]{1,3,2,0:T(8,128)(2,1)S(1)} fusion(bf16[4,512,4,64]{1,3,2,0:T(8,128)(2,1)S(1)} %get-tuple-element.173, s32[]{:T(128)} %get-tuple-element.172, bf16[2048,4,64]{0,2,1:T(8,128)(2,1)} %get-tuple-element.192, f32[4,512,2048]{2,1,0:T(8,128)} %get-tuple-element.157, f32[4,512]{1,0:T(4,128)S(1)} %broadcast_select_fusion.4), kind=kOutput, calls=%fused_computation.17.clone.1 | convolution fusion | flops 545390592 | bytes 18096132 | tf_op jit(solution)/shard_map/while/body/eval_jaxpr/hqk,khd->qhd/dot_general | solution.py:28
  200.0 0.8 copy.14
  200.9 0.3 copy.15
  201.1 3.2 %convolution_convert_fusion = bf16[2048,1024]{1,0:T(8,128)(2,1)} fusion(bf16[2048,256]{0,1:T(8,128)(2,1)S(1)} %bitcast.45, bf16[256,1024]{1,0:T(8,128)(2,1)S(1)} %copy-done), kind=kOutput, calls=%fused_computation.32 | convolution fusion | flops 1075838976 | bytes 5767168 | tf_op jit(solution)/shard_map/dot_general | solution.py:98
  204.4 0.1 convert_reduce_fusion.1
  204.5 0.6 convert_reduce_fusion.3
  205.1 43.8 %reduce-scatter.2.cloned.1.call-done = bf16[2048,256]{1,0:T(8,128)(2,1)} async-done(((bf16[2048,1024]{1,0:T(8,128)(2,1)}), bf16[2048,256]{1,0:T(8,128)(2,1)}) %reduce-scatter.2.cloned.1.call-update) | async-done | bytes 1048592 | tf_op jit(solution)/shard_map/reduce_scatter | solution.py:99
  248.9 2.4 select_reduce_fusion.4
  251.4 22.0 %all-reduce = (f32[256]{0:T(256)S(1)}, f32[]{:T(128)}) all-reduce(f32[256]{0:T(256)S(1)} %get-tuple-element.98, f32[]{:T(128)} %get-tuple-element.96), channel_id=1, replica_groups=mesh['dp'=8,'mp'=4] {'dp'}, use_global_device_ids=true, to_apply=%region_13.15 | all-reduce | flops 257 | bytes 2056 | tf_op jit(solution)/shard_map/psum | solution.py:112
  273.4 0.6 broadcast_divide_fusion
  274.0 0.7 select_convert_fusion
  274.7 2.3 fusion.34
  (40 shorter events, 0.8 us)
Async XLA Ops:
  7.2 194.0 %copy-start = (bf16[256,1024]{1,0:T(8,128)(2,1)S(1)}, bf16[256,1024]{1,0:T(8,128)(2,1)}, u32[]{:S(2)}) copy-start(bf16[256,1024]{1,0:T(8,128)(2,1)} %param.19) | copy-start | bytes 1572868
  10.2 13.7 %all-to-all-start.1 = ((s32[8,16,1]{1,2,0:T(1,128)}), s32[8,16,1]{1,2,0:T(1,128)S(1)}, u32[]{:S(2)}, u32[]{:S(2)}) async-start(s32[8,16,1]{1,2,0:T(1,128)} %bitcast), calls=%async_computation.1 | async-start | bytes 8192 | tf_op jit(solution)/shard_map/all_to_all | solution.py:66
  20.7 33.5 %copy-start.3 = (s32[128]{0:T(128)S(1)}, s32[128]{0:T(128)}, u32[]{:S(2)}) copy-start(s32[128]{0:T(128)} %param.15) | copy-start | bytes 1540
  23.9 28.3 %all-to-all-start = ((bf16[8,256,256]{2,1,0:T(8,128)(2,1)}), bf16[8,256,256]{2,1,0:T(8,128)(2,1)S(1)}, u32[]{:S(2)}, u32[]{:S(2)}) async-start(bf16[8,256,256]{2,1,0:T(8,128)(2,1)} %bitcast.2), calls=%async_computation | async-start | bytes 2097152 | tf_op jit(solution)/shard_map/all_to_all | solution.py:72
  27.5 60.6 %all-gather.2.cloned.1.call-start = ((), (), s32[]{:S(2)}) async-start(), calls=%async_computation.3 | async-start | bytes 5242880 | tf_op jit(solution)/shard_map/all_gather | solution.py:76
  54.1 194.9 %reduce-scatter.2.cloned.1.call-start = ((), (), s32[]{:S(2)}) async-start(), calls=%async_computation.4 | async-start | bytes 5242880 | tf_op jit(solution)/shard_map/reduce_scatter | solution.py:99
  88.1 3.4 %copy-start.1 = (bf16[2048,1024]{1,0:T(8,128)(2,1)S(1)}, bf16[2048,1024]{1,0:T(8,128)(2,1)}, u32[]{:S(2)}) copy-start(bf16[2048,1024]{1,0:T(8,128)(2,1)} %all-gather.2.cloned.1.call-done) | copy-start | bytes 12582916
  92.9 1.2 copy-start.4
  94.1 2.3 copy-start.5
  96.4 2.4 copy-start.6
  204.4 44.6 %copy-start.2 = (bf16[128,16,256]{2,1,0:T(8,128)(2,1)S(1)}, bf16[128,16,256]{2,1,0:T(8,128)(2,1)}, u32[]{:S(2)}) copy-start(bf16[128,16,256]{2,1,0:T(8,128)(2,1)} %broadcast_select_fusion.1) | copy-start | bytes 3145732
Sparse Core Ops, SparseCore 0:
  54.2 33.8 all-gather.1
  204.5 44.3 reduce-scatter.1
where the time goes:
time: 284 us
  waiting for transfers between devices  104 us (37%)
  matrix products  102 us (36%)
  blocking collectives  22 us (8%)
  other arithmetic  18.4 us (6%)
  between operations  14.3 us (5%)
  starting transfers between devices  11 us (4%)
  local copies, waits for them, and re-layouts  9.55 us (3%)
  loops' own time  2.92 us (1%)
    sub x4, matrix products, attend(): raised = jnp.where(allowed[None], jnp.exp(scores - peak), 0.0)  54.1 us
    reduce_scatter x1, waiting for transfers between devices, on_device(): lax.psum_scatter(head_term.astype(jnp.bfloat16), 'mp', scatter_dimension=...  43.8 us
    dot_general x4, matrix products, attend(): jnp.einsum('hqk,khd->qhd', weights, values, preferred_element_type=jnp.fl...  34.9 us
    all_gather x1, waiting for transfers between devices, on_device(): full_rows = lax.all_gather(own_cols, 'mp', axis=1, tiled=True)  33.8 us
    all_to_all x1, waiting for transfers between devices, on_device(): lax.all_to_all(outgoing, 'dp', split_axis=0, concat_axis=0, tiled=True)  23.3 us
    psum x1, blocking collectives, on_device(): grand_total, number = lax.psum((local_sum, local_count), 'dp')  22 us
    all_to_all x1, starting transfers between devices, on_device(): lax.all_to_all(slot_sent, 'dp', split_axis=0, concat_axis=0, tiled=True)  7.31 us
  transfers between devices with their start and end apart: 4, of which 4 were waited for; matrix products, arithmetic and copies ran while one was open for 2% of the time, Pallas kernels for 0%

commit v1 on v0

--- a/solution.py
+++ b/solution.py
@@ -6,6 +6,21 @@
 HEAD_DIM = 64
 IMG_OWN = 16
 EPSILON = 1e-06
+
+
+def time_ratios(z_in, shard_axis):
+    sides = lax.psum(1, shard_axis)
+    local_next = range(sides)
+    new = map(lambda i: (i, (i + 1) % sides), local_next)
+    views = list(new)
+    v1 = [None] * sides
+    v1[sides - 1] = z_in
+    for num in range(sides - 2, -1, -1):
+        v1[num] = lax.ppermute(v1[num + 1], shard_axis, views)
+    g_now = jnp.concatenate(v1, 1)
+    z_new = lax.axis_index(shard_axis)
+    current_block = (z_new + 1) * z_in.shape[1]
+    return jnp.roll(g_now, current_block, axis=1)
 
 
 def normalize(rows):
@@ -73,7 +88,7 @@
     own_cols = jnp.take(
         incoming.reshape(slot_count, tile_size, part_width), arrive, axis=0
     ).reshape(slot_count * tile_size, part_width)
-    full_rows = lax.all_gather(own_cols, "mp", axis=1, tiled=True)
+    full_rows = time_ratios(own_cols, "mp")
     count_rows = slot_count * tile_size
     segment = jnp.repeat(packed_image, tile_size)
     present = segment >= 0

time: 284 us -> 295 us (1.039)
  waiting for transfers between devices: 104 us -> 112 us
  local copies, waits for them, and re-layouts: 9.55 us -> 14.8 us
  other arithmetic: 18.4 us -> 15.2 us
    ppermute x0 -> x3, waiting for transfers between devices: none -> 42.9 us  [time_ratios(): v1[num] = lax.ppermute(v1[num + 1], shard_axis, views)]
    all_gather x1 -> x0, waiting for transfers between devices: 33.8 us -> none  [on_device(): full_rows = lax.all_gather(own_cols, 'mp', axis=1, tiled=True)]
    unnamed x15 -> x24, local copies, waits for them, and re-layouts: 0.78 us -> 6.19 us
  transfers between devices with their start and end apart: 4 -> 6, of which waited for: 4 -> 6; matrix products, arithmetic and copies ran while one was open for 2% -> 2% of each run, Pallas kernels for 0% -> 0%
where the time goes in v1:
time: 295 us; the launch traced here: 294 us
  waiting for transfers between devices  112 us (38%)
  matrix products  102 us (35%)
  blocking collectives  22 us (7%)
  other arithmetic  15.2 us (5%)
  local copies, waits for them, and re-layouts  14.8 us (5%)
  between operations  14.4 us (5%)
  starting transfers between devices  11 us (4%)
    sub x4, matrix products, attend(): raised = jnp.where(allowed[None], jnp.exp(scores - peak), 0.0)  54.3 us
    ppermute x3, waiting for transfers between devices, time_ratios(): v1[num] = lax.ppermute(v1[num + 1], shard_axis, views)  42.9 us
    reduce_scatter x1, waiting for transfers between devices, on_device(): lax.psum_scatter(head_term.astype(jnp.bfloat16), 'mp', scatter_dimension=...  42.6 us
    dot_general x4, matrix products, attend(): jnp.einsum('hqk,khd->qhd', weights, values, preferred_element_type=jnp.fl...  34.9 us
    all_to_all x1, waiting for transfers between devices, on_device(): lax.all_to_all(outgoing, 'dp', split_axis=0, concat_axis=0, tiled=True)  23.3 us
    psum x1, blocking collectives, on_device(): grand_total, number = lax.psum((local_sum, local_count), 'dp')  22 us
    all_to_all x1, starting transfers between devices, on_device(): lax.all_to_all(slot_sent, 'dp', split_axis=0, concat_axis=0, tiled=True)  7.31 us
    unnamed x24, local copies, waits for them, and re-layouts  6.19 us
  transfers between devices with their start and end apart: 6, of which 6 were waited for; matrix products, arithmetic and copies ran while one was open for 2% of the time, Pallas kernels for 0%

profile of v1, /device:TPU:0, one launch (start us, length us, event | category | flops | bytes accessed | tf_op | source)
XLA Modules:
  0.0 293.8 jit_solution(592984040308212447)
XLA Ops:
  7.2 0.9 convert_reduce_fusion.2
  8.1 0.7 multiply_add_fusion
  8.8 0.8 select_reduce_fusion.2
  9.5 0.7 all_to_all.14
  10.2 7.3 %all-to-all-start.1 = ((s32[8,16,1]{1,2,0:T(1,128)}), s32[8,16,1]{1,2,0:T(1,128)S(1)}, u32[]{:S(2)}, u32[]{:S(2)}) async-start(s32[8,16,1]{1,2,0:T(1,128)} %bitcast), calls=%async_computation.1 | async-start | bytes 8192 | tf_op jit(solution)/shard_map/all_to_all | solution.py:81
  17.6 1.3 constant_dynamic-slice_fusion
  18.9 0.6 gather_fusion
  19.5 1.2 broadcast_select_fusion.2
  20.7 3.2 %all-to-all-done.1 = s32[8,16,1]{1,2,0:T(1,128)S(1)} async-done(((s32[8,16,1]{1,2,0:T(1,128)}), s32[8,16,1]{1,2,0:T(1,128)S(1)}, u32[]{:S(2)}, u32[]{:S(2)}) %all-to-all-start.1) | async-done | bytes 544 | tf_op jit(solution)/shard_map/all_to_all | solution.py:81
  23.9 3.6 %all-to-all-start = ((bf16[8,256,256]{2,1,0:T(8,128)(2,1)}), bf16[8,256,256]{2,1,0:T(8,128)(2,1)S(1)}, u32[]{:S(2)}, u32[]{:S(2)}) async-start(bf16[8,256,256]{2,1,0:T(8,128)(2,1)} %bitcast.2), calls=%async_computation | async-start | bytes 2097152 | tf_op jit(solution)/shard_map/all_to_all | solution.py:87
  27.6 0.5 broadcast.116
  28.1 0.7 reduce.3
  28.8 0.1 select_reduce_fusion.1
  29.0 23.3 %all-to-all-done = bf16[8,256,256]{2,1,0:T(8,128)(2,1)S(1)} async-done(((bf16[8,256,256]{2,1,0:T(8,128)(2,1)}), bf16[8,256,256]{2,1,0:T(8,128)(2,1)S(1)}, u32[]{:S(2)}, u32[]{:S(2)}) %all-to-all-start) | async-done | bytes 1048608 | tf_op jit(solution)/shard_map/all_to_all | solution.py:87
  52.2 0.6 gather_fusion.1
  52.9 0.2 broadcast_select_fusion.1
  53.2 14.2 %collective-permute-done = bf16[2048,256]{1,0:T(8,128)(2,1)S(1)} collective-permute-done((bf16[2048,256]{1,0:T(8,128)(2,1)S(1)}, bf16[2048,256]{1,0:T(8,128)(2,1)S(1)}, u32[]{:S(2)}, u32[]{:S(2)}) %collective-permute-start) | collective-permute-done | bytes 1048608 | tf_op jit(solution)/shard_map/ppermute | solution.py:19
  67.4 14.3 %collective-permute-done.1 = bf16[2048,256]{1,0:T(8,128)(2,1)} collective-permute-done((bf16[2048,256]{1,0:T(8,128)(2,1)S(1)}, bf16[2048,256]{1,0:T(8,128)(2,1)}, u32[]{:S(2)}, u32[]{:S(2)}) %collective-permute-start.1) | collective-permute-done | bytes 1048608 | tf_op jit(solution)/shard_map/ppermute | solution.py:19
  81.8 0.1 reshape.133
  81.9 14.4 %collective-permute-done.2 = bf16[2048,256]{1,0:T(8,128)(2,1)} collective-permute-done((bf16[2048,256]{1,0:T(8,128)(2,1)}, bf16[2048,256]{1,0:T(8,128)(2,1)}, u32[]{:S(2)}, u32[]{:S(2)}) %collective-permute-start.2) | collective-permute-done | bytes 1048608 | tf_op jit(solution)/shard_map/ppermute | solution.py:19
  96.3 1.4 constant_dynamic-update-slice_fusion.7
  97.6 1.4 constant_dynamic-update-slice_fusion.6
  99.0 0.1 constant_dynamic-update-slice_fusion.5
  99.1 0.1 constant_dynamic-update-slice_fusion.4
  99.3 1.4 constant_dynamic-update-slice_fusion.3
  100.7 1.4 constant_dynamic-update-slice_fusion.2
  102.0 0.1 constant_dynamic-update-slice_fusion.1
  102.2 0.1 constant_dynamic-update-slice_fusion
  102.4 0.6 convert_reduce_fusion
  103.0 1.4 fusion.31
  104.4 1.1 fusion.32
  105.6 2.4 convolution_convert_fusion.3
  107.9 2.3 convolution_convert_fusion.2
  110.3 2.3 convolution_convert_fusion.1
  112.6 98.7 %while.11 = (s32[]{:T(128)}, bf16[4,512,4,64]{1,3,2,0:T(8,128)(2,1)S(1)}, s32[4]{0:T(128)S(1)}, s32[2048]{0:T(1024)S(1)}, pred[2048]{0:T(1024)(128)(4,1)S(1)}, /...) while((s32[]{:T(128)}, ...), condition=%wide.region_9.11_spmd.clone, body=%wide.region_6.10_spmd.clone.sunk | while | flops 1646399488 | bytes 40707776 | solution.py:60
  112.6 0.6 dynamic_slice.49
  114.0 0.1 eq.130
  114.1 0.8 compare_and_fusion.4
  114.9 13.5 %fusion.69 = (f32[4,512]{1,0:T(4,128)S(1)}, f32[4,512,2048]{2,1,0:T(8,128)}) fusion(pred[512,2048]{1,0:T(8,128)(4,1)S(1)} %compare_and_fusion.4, bf16[2048,4,64]{0,2,1:T(8,128)(2,1)} %get-tuple-element.191, bf16[2048,4,64]{0,2,1:T(8,128)(2,1)} %get-tuple-element.190, s32[]{:T(128)S(6)} %select_n.119), kind=kOutput, calls=%fused_computation.81.clone.1 | convolution fusion | flops 1098909696 | bytes 21505024 | tf_op jit(solution)/shard_map/while/body/eval_jaxpr/sub | solution.py:39
  128.4 8.7 %fusion.70 = bf16[4,512,4,64]{1,3,2,0:T(8,128)(2,1)S(1)} fusion(bf16[4,512,4,64]{1,3,2,0:T(8,128)(2,1)S(1)} %get-tuple-element.173, s32[]{:T(128)} %get-tuple-element.172, bf16[2048,4,64]{0,2,1:T(8,128)(2,1)} %get-tuple-element.192, f32[4,512,2048]{2,1,0:T(8,128)} %get-tuple-element.157, f32[4,512]{1,0:T(4,128)S(1)} %broadcast_select_fusion.4), kind=kOutput, calls=%fused_computation.17.clone.1 | convolution fusion | flops 545390592 | bytes 18096132 | tf_op jit(solution)/shard_map/while/body/eval_jaxpr/hqk,khd->qhd/dot_general | solution.py:43
  137.2 0.6 dynamic_slice.49
  138.7 0.1 eq.130
  138.8 0.8 compare_and_fusion.4
  139.5 13.7 %fusion.69 = (f32[4,512]{1,0:T(4,128)S(1)}, f32[4,512,2048]{2,1,0:T(8,128)}) fusion(pred[512,2048]{1,0:T(8,128)(4,1)S(1)} %compare_and_fusion.4, bf16[2048,4,64]{0,2,1:T(8,128)(2,1)} %get-tuple-element.191, bf16[2048,4,64]{0,2,1:T(8,128)(2,1)} %get-tuple-element.190, s32[]{:T(128)S(6)} %select_n.119), kind=kOutput, calls=%fused_computation.81.clone.1 | convolution fusion | flops 1098909696 | bytes 21505024 | tf_op jit(solution)/shard_map/while/body/eval_jaxpr/sub | solution.py:39
  153.2 8.7 %fusion.70 = bf16[4,512,4,64]{1,3,2,0:T(8,128)(2,1)S(1)} fusion(bf16[4,512,4,64]{1,3,2,0:T(8,128)(2,1)S(1)} %get-tuple-element.173, s32[]{:T(128)} %get-tuple-element.172, bf16[2048,4,64]{0,2,1:T(8,128)(2,1)} %get-tuple-element.192, f32[4,512,2048]{2,1,0:T(8,128)} %get-tuple-element.157, f32[4,512]{1,0:T(4,128)S(1)} %broadcast_select_fusion.4), kind=kOutput, calls=%fused_computation.17.clone.1 | convolution fusion | flops 545390592 | bytes 18096132 | tf_op jit(solution)/shard_map/while/body/eval_jaxpr/hqk,khd->qhd/dot_general | solution.py:43
  162.0 0.6 dynamic_slice.49
  163.6 0.8 compare_and_fusion.4
  164.3 13.6 %fusion.69 = (f32[4,512]{1,0:T(4,128)S(1)}, f32[4,512,2048]{2,1,0:T(8,128)}) fusion(pred[512,2048]{1,0:T(8,128)(4,1)S(1)} %compare_and_fusion.4, bf16[2048,4,64]{0,2,1:T(8,128)(2,1)} %get-tuple-element.191, bf16[2048,4,64]{0,2,1:T(8,128)(2,1)} %get-tuple-element.190, s32[]{:T(128)S(6)} %select_n.119), kind=kOutput, calls=%fused_computation.81.clone.1 | convolution fusion | flops 1098909696 | bytes 21505024 | tf_op jit(solution)/shard_map/while/body/eval_jaxpr/sub | solution.py:39
  177.9 8.7 %fusion.70 = bf16[4,512,4,64]{1,3,2,0:T(8,128)(2,1)S(1)} fusion(bf16[4,512,4,64]{1,3,2,0:T(8,128)(2,1)S(1)} %get-tuple-element.173, s32[]{:T(128)} %get-tuple-element.172, bf16[2048,4,64]{0,2,1:T(8,128)(2,1)} %get-tuple-element.192, f32[4,512,2048]{2,1,0:T(8,128)} %get-tuple-element.157, f32[4,512]{1,0:T(4,128)S(1)} %broadcast_select_fusion.4), kind=kOutput, calls=%fused_computation.17.clone.1 | convolution fusion | flops 545390592 | bytes 18096132 | tf_op jit(solution)/shard_map/while/body/eval_jaxpr/hqk,khd->qhd/dot_general | solution.py:43
  186.6 0.6 dynamic_slice.49
  188.2 0.8 compare_and_fusion.4
  189.0 13.5 %fusion.69 = (f32[4,512]{1,0:T(4,128)S(1)}, f32[4,512,2048]{2,1,0:T(8,128)}) fusion(pred[512,2048]{1,0:T(8,128)(4,1)S(1)} %compare_and_fusion.4, bf16[2048,4,64]{0,2,1:T(8,128)(2,1)} %get-tuple-element.191, bf16[2048,4,64]{0,2,1:T(8,128)(2,1)} %get-tuple-element.190, s32[]{:T(128)S(6)} %select_n.119), kind=kOutput, calls=%fused_computation.81.clone.1 | convolution fusion | flops 1098909696 | bytes 21505024 | tf_op jit(solution)/shard_map/while/body/eval_jaxpr/sub | solution.py:39
  202.5 8.7 %fusion.70 = bf16[4,512,4,64]{1,3,2,0:T(8,128)(2,1)S(1)} fusion(bf16[4,512,4,64]{1,3,2,0:T(8,128)(2,1)S(1)} %get-tuple-element.173, s32[]{:T(128)} %get-tuple-element.172, bf16[2048,4,64]{0,2,1:T(8,128)(2,1)} %get-tuple-element.192, f32[4,512,2048]{2,1,0:T(8,128)} %get-tuple-element.157, f32[4,512]{1,0:T(4,128)S(1)} %broadcast_select_fusion.4), kind=kOutput, calls=%fused_computation.17.clone.1 | convolution fusion | flops 545390592 | bytes 18096132 | tf_op jit(solution)/shard_map/while/body/eval_jaxpr/hqk,khd->qhd/dot_general | solution.py:43
  211.2 0.8 copy.14
  212.1 0.3 copy.15
  212.3 3.2 %convolution_convert_fusion = bf16[2048,1024]{1,0:T(8,128)(2,1)} fusion(bf16[2048,256]{0,1:T(8,128)(2,1)S(1)} %bitcast.47, bf16[256,1024]{1,0:T(8,128)(2,1)S(1)} %copy-done), kind=kOutput, calls=%fused_computation.32 | convolution fusion | flops 1075838976 | bytes 5767168 | tf_op jit(solution)/shard_map/dot_general | solution.py:113
  215.6 0.1 convert_reduce_fusion.1
  215.7 0.6 convert_reduce_fusion.3
  216.3 42.6 %reduce-scatter.2.cloned.1.call-done = bf16[2048,256]{1,0:T(8,128)(2,1)} async-done(((bf16[2048,1024]{1,0:T(8,128)(2,1)}), bf16[2048,256]{1,0:T(8,128)(2,1)}) %reduce-scatter.2.cloned.1.call-update) | async-done | bytes 1048592 | tf_op jit(solution)/shard_map/reduce_scatter | solution.py:114
  259.0 2.4 select_reduce_fusion.4
  261.4 22.0 %all-reduce = (f32[256]{0:T(256)S(1)}, f32[]{:T(128)}) all-reduce(f32[256]{0:T(256)S(1)} %get-tuple-element.98, f32[]{:T(128)} %get-tuple-element.96), channel_id=1, replica_groups=mesh['dp'=8,'mp'=4] {'dp'}, use_global_device_ids=true, to_apply=%region_13.15 | all-reduce | flops 257 | bytes 2056 | tf_op jit(solution)/shard_map/psum | solution.py:127
  283.4 0.6 broadcast_divide_fusion
  284.1 0.7 select_convert_fusion
  284.7 2.3 fusion.34
  (53 shorter events, 1.5 us)
Async XLA Ops:
  7.2 205.2 %copy-start = (bf16[256,1024]{1,0:T(8,128)(2,1)S(1)}, bf16[256,1024]{1,0:T(8,128)(2,1)}, u32[]{:S(2)}) copy-start(bf16[256,1024]{1,0:T(8,128)(2,1)} %param.19) | copy-start | bytes 1572868
  7.2 74.5 %copy-start.4 = (s32[128]{0:T(128)S(1)}, s32[128]{0:T(128)}, u32[]{:S(2)}) copy-start(s32[128]{0:T(128)} %param.15) | copy-start | bytes 1540
  10.2 13.7 %all-to-all-start.1 = ((s32[8,16,1]{1,2,0:T(1,128)}), s32[8,16,1]{1,2,0:T(1,128)S(1)}, u32[]{:S(2)}, u32[]{:S(2)}) async-start(s32[8,16,1]{1,2,0:T(1,128)} %bitcast), calls=%async_computation.1 | async-start | bytes 8192 | tf_op jit(solution)/shard_map/all_to_all | solution.py:81
  23.9 28.3 %all-to-all-start = ((bf16[8,256,256]{2,1,0:T(8,128)(2,1)}), bf16[8,256,256]{2,1,0:T(8,128)(2,1)S(1)}, u32[]{:S(2)}, u32[]{:S(2)}) async-start(bf16[8,256,256]{2,1,0:T(8,128)(2,1)} %bitcast.2), calls=%async_computation | async-start | bytes 2097152 | tf_op jit(solution)/shard_map/all_to_all | solution.py:87
  27.5 231.5 %reduce-scatter.2.cloned.1.call-start = ((), (), s32[]{:S(2)}) async-start(), calls=%async_computation.3 | async-start | bytes 5242880 | tf_op jit(solution)/shard_map/reduce_scatter | solution.py:114
  53.1 49.2 %copy-start.1 = (bf16[128,16,256]{2,1,0:T(8,128)(2,1)}, bf16[128,16,256]{2,1,0:T(8,128)(2,1)S(1)}, u32[]{:S(2)}) copy-start(bf16[128,16,256]{2,1,0:T(8,128)(2,1)S(1)} %broadcast_select_fusion.1) | copy-start | bytes 3145732
  53.1 14.3 %collective-permute-start = (bf16[2048,256]{1,0:T(8,128)(2,1)S(1)}, bf16[2048,256]{1,0:T(8,128)(2,1)S(1)}, u32[]{:S(2)}, u32[]{:S(2)}) collective-permute-start(bf16[2048,256]{1,0:T(8,128)(2,1)S(1)} %bitcast.43), channel_id=1, source_target_pairs={{0,1},{1,2},{2,3},{3,0},{4,5},{5,6},{6,7},{7,4},{8,9},{9,10},{10,1... | collective-permute-start | bytes 3145736 | tf_op jit(solution)/shard_map/ppermute | solution.py:19
  67.4 14.3 %collective-permute-start.1 = (bf16[2048,256]{1,0:T(8,128)(2,1)S(1)}, bf16[2048,256]{1,0:T(8,128)(2,1)}, u32[]{:S(2)}, u32[]{:S(2)}) collective-permute-start(bf16[2048,256]{1,0:T(8,128)(2,1)S(1)} %collective-permute-done), channel_id=1, source_target_pairs={{0,1},{1,2},{2,3},{3,0},{4,5},{5,6},{6,7},{7,4},{8,9},{9,10},{10,1... | collective-permute-start | bytes 3145736 | tf_op jit(solution)/shard_map/ppermute | solution.py:19
  81.7 14.5 %collective-permute-start.2 = (bf16[2048,256]{1,0:T(8,128)(2,1)}, bf16[2048,256]{1,0:T(8,128)(2,1)}, u32[]{:S(2)}, u32[]{:S(2)}) collective-permute-start(bf16[2048,256]{1,0:T(8,128)(2,1)} %collective-permute-done.1), channel_id=1, source_target_pairs={{0,1},{1,2},{2,3},{3,0},{4,5},{5,6},{6,7},{7,4},{8,9},{9,10},{10,1... | collective-permute-start | bytes 3145736 | tf_op jit(solution)/shard_map/ppermute | solution.py:19
  102.4 3.2 %copy-start.5 = (bf16[1024,256]{1,0:T(8,128)(2,1)S(1)}, bf16[1024,256]{1,0:T(8,128)(2,1)}, u32[]{:S(2)}) copy-start(bf16[1024,256]{1,0:T(8,128)(2,1)} %param.16) | copy-start | bytes 1572868
  104.4 3.5 %copy-start.6 = (bf16[1024,256]{1,0:T(8,128)(2,1)S(1)}, bf16[1024,256]{1,0:T(8,128)(2,1)}, u32[]{:S(2)}) copy-start(bf16[1024,256]{1,0:T(8,128)(2,1)} %param.17) | copy-start | bytes 1572868
  107.9 2.3 copy-start.7
  110.3 2.3 copy-start.3
  211.2 47.7 %copy-start.2 = (bf16[128,16,256]{2,1,0:T(8,128)(2,1)S(1)}, bf16[128,16,256]{2,1,0:T(8,128)(2,1)}, u32[]{:S(2)}) copy-start(bf16[128,16,256]{2,1,0:T(8,128)(2,1)} %copy-done.1) | copy-start | bytes 3145732
Sparse Core Ops, SparseCore 0:
  215.7 43.2 reduce-scatter.1
